TPU v7x, 32 devices: a whole 2x2x4 slice. The times are simulated.
32 devices in a mesh: lat: 8 (over z, y), grp: 4 (over x, core).
Axes of the slice: x: 2, y: 2, z: 4, core: 2. Of those that a mesh axis runs over, the one named last changes fastest.
Arguments:
- tokens: bfloat16 [384, 64, 1024], P('grp', 'lat'), may hold values from -6 to 6
- cotangent: bfloat16 [384, 64, 1024], P('grp', 'lat'), may hold values from -6 to 6
- gain: float32 [384], P('grp'), may hold values from 0.5 to 1.5
- shift: float32 [384], P('grp'), may hold values from -3 to 3
- w_in: float32 [4, 2, 96, 96], P('grp'), may hold values from -0.4375 to 0.4375
- b_in: float32 [4, 2, 96], P('grp'), may hold values from -0.3 to 0.3
- w_out: float32 [4, 2, 96, 96], P('grp'), may hold values from -0.4375 to 0.4375
- b_out: float32 [4, 2, 96], P('grp'), may hold values from -0.12 to 0.12
Outputs:
- mixed: bfloat16 [384, 64, 1024], P('grp', 'lat')
- grad_tokens: bfloat16 [384, 64, 1024], P('grp', 'lat')
- grad_weights: float32 [4, 36864], P('grp', 'lat')
All inputs are finite; a program needn't handle non-finite values.
Results may differ from a plain program's by a relative error of at most 0.012.
Values sent between devices are 32-bit elements; how exact they have to be, the bound alone decides.
A program may use at most 128 MiB of HBM per device.

v0:
```python
import math
import jax
import jax.numpy as jnp
from jax import lax
from jax.sharding import PartitionSpec as P

highest = lax.Precision.HIGHEST
shrink_level = 0.01
norm_eps = 1e-05


def contract(form, left, right):
    return jnp.einsum(form, left, right, precision=highest)


def angle_table(left_count, right_count, length):
    left_index = jnp.arange(left_count, dtype=jnp.int32)[:, None]
    right_index = jnp.arange(right_count, dtype=jnp.int32)[None, :]
    phase = left_index * right_index % length
    theta = phase.astype(jnp.float32) * (2.0 * math.pi / length)
    return (jnp.cos(theta), jnp.sin(theta))


def lon_forward(field, modes):
    length = field.shape[2]
    cos_tab, sin_tab = angle_table(length, modes, length)
    scale = 1.0 / math.sqrt(length)
    out_real = contract("crn,nm->cmr", field, cos_tab) * scale
    out_imag = contract("crn,nm->cmr", field, sin_tab) * -scale
    return jnp.stack([out_real, out_imag])


def lon_inverse(stack, length, weighted):
    modes = stack.shape[2]
    cos_tab, sin_tab = angle_table(modes, length, length)
    scale = 1.0 / math.sqrt(length)
    real_part = stack[0]
    imag_part = stack[1]
    if weighted:
        mode_weight = jnp.where(jnp.arange(modes) == 0, 1.0, 2.0).astype(jnp.float32)[None, :, None]
        real_part = real_part * mode_weight
        imag_part = imag_part * mode_weight
    out = contract("cmr,mn->crn", real_part, cos_tab) - contract("cmr,mn->crn", imag_part, sin_tab)
    return out * scale


def lat_forward(stack):
    real_part, imag_part = (stack[0], stack[1])
    length = real_part.shape[-1]
    cos_tab, sin_tab = angle_table(length, length, length)
    scale = 1.0 / math.sqrt(length)
    out_real = contract("cql,lk->cqk", real_part, cos_tab) + contract(
        "cql,lk->cqk", imag_part, sin_tab
    )
    out_imag = contract("cql,lk->cqk", imag_part, cos_tab) - contract(
        "cql,lk->cqk", real_part, sin_tab
    )
    return (out_real * scale, out_imag * scale)


def lat_inverse(real_part, imag_part):
    length = real_part.shape[-1]
    cos_tab, sin_tab = angle_table(length, length, length)
    scale = 1.0 / math.sqrt(length)
    out_real = contract("cql,lk->cqk", real_part, cos_tab) - contract(
        "cql,lk->cqk", imag_part, sin_tab
    )
    out_imag = contract("cql,lk->cqk", imag_part, cos_tab) + contract(
        "cql,lk->cqk", real_part, sin_tab
    )
    return jnp.stack([out_real * scale, out_imag * scale])


def complex_mix(left_real, left_imag, weight):
    form = "bihk,bio->bohk"
    w_real = weight[:, 0]
    w_imag = weight[:, 1]
    out_real = contract(form, left_real, w_real) - contract(form, left_imag, w_imag)
    out_imag = contract(form, left_imag, w_real) + contract(form, left_real, w_imag)
    return (out_real, out_imag)


def mix_back(grad_real, grad_imag, weight):
    form = "bohk,bio->bihk"
    w_real = weight[:, 0]
    w_imag = weight[:, 1]
    back_real = contract(form, grad_real, w_real) + contract(form, grad_imag, w_imag)
    back_imag = contract(form, grad_imag, w_real) - contract(form, grad_real, w_imag)
    return (back_real, back_imag)


def weight_grad(left_real, left_imag, grad_real, grad_imag):
    form = "bihk,bohk->bio"
    grad_wreal = contract(form, left_real, grad_real) + contract(form, left_imag, grad_imag)
    grad_wimag = contract(form, left_real, grad_imag) - contract(form, left_imag, grad_real)
    return (grad_wreal, grad_wimag)


def shrink(value):
    return jnp.sign(value) * jnp.maximum(jnp.abs(value) - shrink_level, 0.0)


def regroup_modes(parts, lat_count, grp_count):
    _, two, chans, quarter, rows = parts.shape
    split = parts.reshape(lat_count, grp_count, two, chans, quarter, rows)
    split = jnp.transpose(split, (2, 1, 3, 4, 0, 5))
    return split.reshape(two, grp_count * chans, quarter, lat_count * rows)


def regroup_rows(stack, lat_count, grp_count, chans):
    two, _, quarter, lat_len = stack.shape
    rows = lat_len // lat_count
    split = stack.reshape(two, grp_count, chans, quarter, lat_count, rows)
    split = jnp.transpose(split, (4, 1, 0, 2, 3, 5))
    return split.reshape(lat_count * grp_count, two, chans, quarter, rows)


def per_device(tokens, cotangent, gain, shift, w_in, b_in, w_out, b_out):
    chans, rows, length = tokens.shape
    lat_count = lax.axis_size("lat")
    grp_count = lax.axis_size("grp")
    all_chans = chans * grp_count
    modes = length // 2
    tok_val = tokens.astype(jnp.float32)
    grad_val = cotangent.astype(jnp.float32)
    first_sum, second_sum = lax.psum(
        (jnp.sum(tok_val, axis=0), jnp.sum(tok_val * tok_val, axis=0)), "grp"
    )
    token_mean = first_sum / all_chans
    inv_std = lax.rsqrt(second_sum / all_chans - token_mean * token_mean + norm_eps)
    normed = (tok_val - token_mean) * inv_std
    normal_out = normed * gain[:, None, None] + shift[:, None, None]
    mode_weight = jnp.where(jnp.arange(modes) == 0, 1.0, 2.0).astype(jnp.float32)[
        None, None, :, None
    ]
    spec_field = lon_forward(normal_out, modes)
    spec_grad = lon_forward(grad_val, modes) * mode_weight
    parts_field, parts_grad = (
        lax.all_to_all(spec_field[None], ("lat", "grp"), split_axis=3, concat_axis=0, tiled=True),
        lax.all_to_all(spec_grad[None], ("lat", "grp"), split_axis=3, concat_axis=0, tiled=True),
    )
    modes_field = regroup_modes(parts_field, lat_count, grp_count)
    modes_grad = regroup_modes(parts_grad, lat_count, grp_count)
    block_in, bias_in, block_out, bias_out = (
        lax.all_gather(w_in, "grp", axis=0, tiled=True),
        lax.all_gather(b_in, "grp", axis=0, tiled=True),
        lax.all_gather(w_out, "grp", axis=0, tiled=True),
        lax.all_gather(b_out, "grp", axis=0, tiled=True),
    )
    block_count = block_in.shape[0]
    block_size = block_in.shape[2]
    quarter = modes_field.shape[2]
    lat_len = modes_field.shape[3]
    spec_real, spec_imag = lat_forward(modes_field)
    grad_real, grad_imag = lat_forward(modes_grad)
    blocked = (block_count, block_size, quarter, lat_len)
    spec_real = spec_real.reshape(blocked)
    spec_imag = spec_imag.reshape(blocked)
    grad_real = grad_real.reshape(blocked)
    grad_imag = grad_imag.reshape(blocked)
    pre_real, pre_imag = complex_mix(spec_real, spec_imag, block_in)
    pre_real = pre_real + bias_in[:, 0, :, None, None]
    pre_imag = pre_imag + bias_in[:, 1, :, None, None]
    act_real = jax.nn.relu(pre_real)
    act_imag = jax.nn.relu(pre_imag)
    post_real, post_imag = complex_mix(act_real, act_imag, block_out)
    post_real = post_real + bias_out[:, 0, :, None, None]
    post_imag = post_imag + bias_out[:, 1, :, None, None]
    shrunk_real = shrink(post_real)
    shrunk_imag = shrink(post_imag)
    d_post_real = jnp.where(jnp.abs(post_real) > shrink_level, grad_real, 0.0)
    d_post_imag = jnp.where(jnp.abs(post_imag) > shrink_level, grad_imag, 0.0)
    g_out_real, g_out_imag = weight_grad(act_real, act_imag, d_post_real, d_post_imag)
    d_act_real, d_act_imag = mix_back(d_post_real, d_post_imag, block_out)
    d_pre_real = jnp.where(pre_real > 0.0, d_act_real, 0.0)
    d_pre_imag = jnp.where(pre_imag > 0.0, d_act_imag, 0.0)
    g_in_real, g_in_imag = weight_grad(spec_real, spec_imag, d_pre_real, d_pre_imag)
    d_spec_real, d_spec_imag = mix_back(d_pre_real, d_pre_imag, block_in)
    flat_shape = (block_count * block_size, quarter, lat_len)
    back_field = lat_inverse(shrunk_real.reshape(flat_shape), shrunk_imag.reshape(flat_shape))
    back_grad = lat_inverse(d_spec_real.reshape(flat_shape), d_spec_imag.reshape(flat_shape))
    grad_stack = jnp.stack([g_in_real, g_in_imag, g_out_real, g_out_imag], axis=1)
    grad_term = grad_stack.reshape(block_count, 4 * block_size * block_size) * (
        1.0 / math.sqrt(lat_len * modes)
    )
    send_field = regroup_rows(back_field, lat_count, grp_count, chans)
    send_grad = regroup_rows(back_grad, lat_count, grp_count, chans)
    rows_field, rows_grad = (
        lax.all_to_all(send_field, ("lat", "grp"), split_axis=0, concat_axis=3, tiled=True),
        lax.all_to_all(send_grad, ("lat", "grp"), split_axis=0, concat_axis=3, tiled=True),
    )
    rows_field = rows_field[0]
    rows_grad = rows_grad[0]
    piece = grad_term.shape[1] // lat_count
    ordered = jnp.transpose(grad_term.reshape(block_count, lat_count, piece), (1, 0, 2))
    grad_weights = lax.psum_scatter(
        ordered.reshape(lat_count * block_count, piece),
        ("lat", "grp"),
        scatter_dimension=0,
        tiled=True,
    )
    filtered = lon_inverse(rows_field, length, True)
    pulled = lon_inverse(rows_grad, length, False)
    mixed = (filtered + normal_out + tok_val).astype(jnp.bfloat16)
    d_normal = grad_val + pulled
    dnorm = d_normal * gain[:, None, None]
    back_one, back_two = lax.psum((jnp.sum(dnorm, axis=0), jnp.sum(dnorm * normed, axis=0)), "grp")
    grad_tokens = grad_val + inv_std * (
        dnorm - back_one / all_chans - normed * (back_two / all_chans)
    )
    return (mixed, grad_tokens.astype(jnp.bfloat16), grad_weights)


def solution(mesh):
    in_specs = (
        P("grp", "lat", None),
        P("grp", "lat", None),
        P("grp"),
        P("grp"),
        P("grp", None, None, None),
        P("grp", None, None),
        P("grp", None, None, None),
        P("grp", None, None),
    )
    out_specs = (P("grp", "lat", None), P("grp", "lat", None), P("grp", "lat"))
    return jax.shard_map(
        per_device, mesh=mesh, in_specs=in_specs, out_specs=out_specs, check_vma=False
    )
```

profile of v0, /device:TPU:0, one launch (start us, length us, event | category | flops | bytes accessed | tf_op | source)
XLA Modules:
  0.0 715.0 jit_solution(96283752565888602)
XLA Ops:
  7.2 12.5 %multiply_bitcast_fusion.2 = f32[1,1,96,512,8]{3,2,4,1,0:T(8,128)S(1)} fusion(bf16[96,8,1024]{2,1,0:T(8,128)(2,1)} %param.9), kind=kOutput, calls=%fused_computation.130 | convolution fusion | flops 4839571456 | bytes 3145728 | tf_op jit(solution)/shard_map/crn,nm->cmr/dot_general | solution.py:13
  19.7 11.4 %multiply_bitcast_fusion.3 = f32[1,1,96,512,8]{3,2,4,1,0:T(8,128)S(1)} fusion(bf16[96,8,1024]{2,1,0:T(8,128)(2,1)S(1)} %copy-done.30), kind=kOutput, calls=%fused_computation.131 | convolution fusion | flops 4839571456 | bytes 3145728 | tf_op jit(solution)/shard_map/crn,nm->cmr/dot_general | solution.py:13
  31.5 3.5 copy.115
  35.1 7.5 %all-to-all-start.2 = ((f32[1,2,96,512,8]{2,4,1,0,3:T(8,128)}), f32[1,2,96,512,8]{2,4,1,0,3:T(8,128)}, u32[]{:S(2)}, u32[]{:S(2)}) async-start(f32[1,2,96,512,8]{2,4,1,0,3:T(8,128)} %copy.115), calls=%async_computation.2 | async-start | bytes 8388608 | tf_op jit(solution)/shard_map/all_to_all | solution.py:140
  43.9 41.2 %all-reduce.11.cloned.1.call-done = (f32[8,1024]{1,0:T(8,128)}, f32[8,1024]{1,0:T(8,128)}) async-done(((f32[8,1024]{1,0:T(8,128)}, f32[8,1024]{1,0:T(8,128)}), (f32[8,1024]{1,0:T(8,128)}, f32[8,1024]{1,0:T(8,128)})) %all-reduce.11.cloned.1.call-update) | async-done | bytes 65552 | tf_op jit(solution)/shard_map/psum | solution.py:126
  87.0 14.2 %multiply_bitcast_fusion.4 = f32[1,96,512,8]{2,1,3,0:T(8,128)S(1)} fusion(f32[96,8,1024]{2,1,0:T(8,128)S(1)} %fusion.6), kind=kOutput, calls=%fused_computation.136 | convolution fusion | flops 4839571456 | bytes 4718592 | tf_op jit(solution)/shard_map/crn,nm->cmr/dot_general | solution.py:13
  101.2 13.8 %multiply_bitcast_fusion.5 = f32[1,96,512,8]{2,1,3,0:T(8,128)S(1)} fusion(f32[96,8,1024]{2,1,0:T(8,128)S(1)} %fusion.6), kind=kOutput, calls=%fused_computation.137 | convolution fusion | flops 4839571456 | bytes 4718592 | tf_op jit(solution)/shard_map/crn,nm->cmr/dot_general | solution.py:13
  115.3 3.6 copy.98
  118.9 17.3 %all-to-all-done.2 = f32[1,2,96,512,8]{2,4,1,0,3:T(8,128)} async-done(((f32[1,2,96,512,8]{2,4,1,0,3:T(8,128)}), f32[1,2,96,512,8]{2,4,1,0,3:T(8,128)}, u32[]{:S(2)}, u32[]{:S(2)}) %all-to-all-start.2) | async-done | bytes 3145760 | tf_op jit(solution)/shard_map/all_to_all | solution.py:140
  136.2 4.2 all-to-all-start
  140.5 27.9 %all_gather.13 = f32[4,2,96]{2,1,0:T(2,128)S(1)} all-gather(f32[1,2,96]{2,1,0:T(2,128)S(1)} %copy-done.39), channel_id=1, replica_groups=mesh['lat'=8,'grp'=4] {'grp'}, dimensions={0}, use_global_device_ids=true | all-gather | bytes 3840 | tf_op jit(solution)/shard_map/all_gather | solution.py:146
  168.4 5.7 all_gather.15
  174.1 6.7 all_gather.12
  180.7 13.8 %all_gather.14 = f32[4,2,96,96]{3,2,0,1:T(8,128)} all-gather(f32[1,2,96,96]{3,2,0,1:T(8,128)S(1)} %bitcast.375), channel_id=1, replica_groups=mesh['lat'=8,'grp'=4] {'grp'}, dimensions={0}, use_global_device_ids=true | all-gather | bytes 368640 | tf_op jit(solution)/shard_map/all_gather | solution.py:147
  195.2 4.9 copy.198
  212.2 3.6 reshape.140
  221.7 12.5 %all-to-all-done = f32[1,2,96,512,8]{2,4,1,0,3:T(8,128)} async-done(((f32[1,2,96,512,8]{2,4,1,0,3:T(8,128)}), f32[1,2,96,512,8]{2,4,1,0,3:T(8,128)}, u32[]{:S(2)}, u32[]{:S(2)}) %all-to-all-start) | async-done | bytes 3145760 | tf_op jit(solution)/shard_map/all_to_all | solution.py:139
  234.2 4.9 copy.199
  266.6 3.3 fusion.52
  274.3 3.8 copy_select_fusion
  284.8 6.5 copy_select_fusion.1
  294.8 3.6 reshape.136
  309.0 3.5 stack.55
  315.7 3.5 stack.54
  323.7 4.4 all-to-all-start.1
  328.2 3.7 fusion.208
  350.2 3.7 fusion.28
  358.6 3.6 reshape.142
  368.2 3.5 stack.61
  379.5 3.5 stack.60
  387.7 34.0 %all-to-all-done.1 = f32[32,2,96,16,8]{2,4,3,1,0:T(8,128)} async-done(((f32[32,2,96,16,8]{2,4,3,1,0:T(8,128)}), f32[32,2,96,16,8]{2,4,3,1,0:T(8,128)}, u32[]{:S(2)}, u32[]{:S(2)}) %all-to-all-start.1) | async-done | bytes 3145760 | tf_op jit(solution)/shard_map/all_to_all | solution.py:189
  421.7 4.2 all-to-all-start.3
  426.2 5.8 fusion.127
  432.1 3.5 fusion.124
  435.6 3.4 fusion.136
  439.0 3.8 fusion.141
  442.9 3.5 fusion.159
  446.4 3.5 fusion.165
  449.9 3.6 fusion.183
  453.6 3.4 fusion.173
  459.0 143.5 %all-reduce.7.cloned.1.call-done = f32[32,4608]{1,0:T(8,128)} async-done(((f32[32,4608]{1,0:T(8,128)}), f32[32,4608]{1,0:T(8,128)}) %all-reduce.7.cloned.1.call-update) | async-done | bytes 589840
  614.1 15.6 %fusion.40 = f32[96,8,1024]{2,1,0:T(8,128)} fusion(f32[96,512,8]{1,2,0:T(8,128)} %copy.112), kind=kOutput, calls=%fused_computation.58 | convolution fusion | flops 4839178240 | bytes 4718592 | tf_op jit(solution)/shard_map/cmr,mn->crn/dot_general | solution.py:13
  629.6 3.9 fusion.364
  638.5 16.3 %fusion.38 = f32[96,8,1024]{2,1,0:T(8,128)S(1)} fusion(f32[96,512,8]{1,2,0:T(8,128)} %copy.125), kind=kOutput, calls=%fused_computation.56 | convolution fusion | flops 4839178240 | bytes 4718592 | tf_op jit(solution)/shard_map/cmr,mn->crn/dot_general | solution.py:13
  654.8 15.9 %fusion.363 = (f32[8,1024]{1,0:T(8,128)}, f32[8,1024]{1,0:T(8,128)}, f32[96,8,1024]{2,1,0:T(8,128)}) fusion(f32[8,1024]{1,0:T(8,128)S(1)} %copy-done.35, f32[8,1024]{1,0:T(8,128)S(1)} %copy-done.33, bf16[96,8,1024]{2,1,0:T(8,128)(2,1)S(1)} %copy-done.23, f32[96]{0:T(128)S(1)} %copy-done.44, f32[96,8,1024]{2,1,0:T(8,128)S(1)} %fusion.38, ...), kind=kOutput, calls=%fused_computation.321 | convolution fusion | flops 4847812608 | bytes 11141504 | tf_op jit(solution)/shard_map/cmr,mn->crn/dot_general | solution.py:13
  670.8 16.3 %fusion.11 = bf16[96,8,1024]{2,1,0:T(8,128)(2,1)} fusion(bf16[96,8,1024]{2,1,0:T(8,128)(2,1)S(1)} %copy-done.23, f32[96,8,1024]{2,1,0:T(8,128)} %fusion.40, f32[96,512,8]{1,2,0:T(8,128)S(1)} %copy-done.28, f32[96]{0:T(128)S(1)} %copy-done.42, f32[96]{0:T(128)S(1)} %copy-done.44, f32[8,1024]{1,0:T(8,128)S(1)} %copy-done.35, f32[8,1024]{1,0:T(8,128)S(1)} %copy-done.33), kind=kOutput, calls=%fused_computation.21 | convolution fusion | flops 4847042560 | bytes 7930624 | tf_op jit(solution)/shard_map/cmr,mn->crn/dot_general | solution.py:13
  687.0 15.7 %all-reduce.9.cloned.1.call-done = (f32[8,1024]{1,0:T(8,128)}, f32[8,1024]{1,0:T(8,128)}) async-done(((f32[8,1024]{1,0:T(8,128)}, f32[8,1024]{1,0:T(8,128)}), (f32[8,1024]{1,0:T(8,128)}, f32[8,1024]{1,0:T(8,128)})) %all-reduce.9.cloned.1.call-update) | async-done | bytes 65552 | tf_op jit(solution)/shard_map/psum | solution.py:207
  703.5 4.5 fusion.1
  (168 shorter events, 143.5 us)
Async XLA Ops:
  7.2 12.5 %copy-start.30 = (bf16[96,8,1024]{2,1,0:T(8,128)(2,1)S(1)}, bf16[96,8,1024]{2,1,0:T(8,128)(2,1)}, u32[]{:S(2)}) copy-start(bf16[96,8,1024]{2,1,0:T(8,128)(2,1)} %param.9) | copy-start | bytes 4718596
  35.1 7.7 %copy-start.22 = (bf16[96,8,1024]{2,1,0:T(8,128)(2,1)S(1)}, bf16[96,8,1024]{2,1,0:T(8,128)(2,1)}, u32[]{:S(2)}) copy-start(bf16[96,8,1024]{2,1,0:T(8,128)(2,1)} %param.8) | copy-start | bytes 4718596
  35.1 51.4 %copy-start.41 = (f32[96]{0:T(128)S(1)}, f32[96]{0:T(128)}, u32[]{:S(2)}) copy-start(f32[96]{0:T(128)} %param.11) | copy-start | bytes 1156
  35.1 51.4 %copy-start.43 = (f32[96]{0:T(128)S(1)}, f32[96]{0:T(128)}, u32[]{:S(2)}) copy-start(f32[96]{0:T(128)} %param.10) | copy-start | bytes 1156
  35.1 101.2 %all-to-all-start.2 = ((f32[1,2,96,512,8]{2,4,1,0,3:T(8,128)}), f32[1,2,96,512,8]{2,4,1,0,3:T(8,128)}, u32[]{:S(2)}, u32[]{:S(2)}) async-start(f32[1,2,96,512,8]{2,4,1,0,3:T(8,128)} %copy.115), calls=%async_computation.2 | async-start | bytes 8388608 | tf_op jit(solution)/shard_map/all_to_all | solution.py:140
  42.5 42.5 %all-reduce.11.cloned.1.call-start = ((), (), s32[]{:S(2)}) async-start(), calls=%async_computation.6 | async-start | bytes 131072 | tf_op jit(solution)/shard_map/psum | solution.py:126
  118.9 21.6 %copy-start.39 = (f32[1,2,96]{2,1,0:T(2,128)S(1)}, f32[1,2,96]{2,1,0:T(2,128)}, u32[]{:S(2)}) copy-start(f32[1,2,96]{2,1,0:T(2,128)} %param.13) | copy-start | bytes 2308
  118.9 49.5 %copy-start.40 = (f32[1,2,96]{2,1,0:T(2,128)S(1)}, f32[1,2,96]{2,1,0:T(2,128)}, u32[]{:S(2)}) copy-start(f32[1,2,96]{2,1,0:T(2,128)} %param.15) | copy-start | bytes 2308
  118.9 55.2 %copy-start.36 = (f32[1,2,96,96]{3,2,1,0:T(8,128)S(1)}, f32[1,2,96,96]{3,2,1,0:T(8,128)}, u32[]{:S(2)}) copy-start(f32[1,2,96,96]{3,2,1,0:T(8,128)} %param.12) | copy-start | bytes 221188
  118.9 61.8 %copy-start.37 = (f32[1,2,96,96]{3,2,1,0:T(8,128)S(1)}, f32[1,2,96,96]{3,2,1,0:T(8,128)}, u32[]{:S(2)}) copy-start(f32[1,2,96,96]{3,2,1,0:T(8,128)} %param.14) | copy-start | bytes 221188
  136.2 97.9 %all-to-all-start = ((f32[1,2,96,512,8]{2,4,1,0,3:T(8,128)}), f32[1,2,96,512,8]{2,4,1,0,3:T(8,128)}, u32[]{:S(2)}, u32[]{:S(2)}) async-start(f32[1,2,96,512,8]{2,4,1,0,3:T(8,128)} %copy.98), calls=%async_computation | async-start | bytes 8388608 | tf_op jit(solution)/shard_map/all_to_all | solution.py:139
  260.1 2.0 copy-start.5
  260.1 2.3 copy-start.3
  260.1 2.3 copy-start.38
  262.4 2.1 copy-start.24
  266.6 3.3 copy-start.6
  271.9 2.4 copy-start.25
  274.3 3.8 copy-start
  298.4 3.2 copy-start.18
  303.2 2.9 copy-start.21
  319.2 2.2 copy-start.27
  323.7 98.0 %all-to-all-start.1 = ((f32[32,2,96,16,8]{2,4,3,1,0:T(8,128)}), f32[32,2,96,16,8]{2,4,3,1,0:T(8,128)}, u32[]{:S(2)}, u32[]{:S(2)}) async-start(f32[32,2,96,16,8]{2,4,3,1,0:T(8,128)} %bitcast.368), calls=%async_computation.1 | async-start | bytes 8388608 | tf_op jit(solution)/shard_map/all_to_all | solution.py:189
  328.2 3.7 copy-start.15
  337.5 2.0 copy-start.1
  337.5 2.2 copy-start.13
  342.0 2.3 copy-start.8
  350.2 3.7 copy-start.9
  362.2 3.2 copy-start.19
  371.7 3.3 copy-start.20
  383.0 2.2 copy-start.26
  421.7 208.0 %all-to-all-start.3 = ((f32[32,2,96,16,8]{2,4,3,1,0:T(8,128)}), f32[32,2,96,16,8]{2,4,3,1,0:T(8,128)}, u32[]{:S(2)}, u32[]{:S(2)}) async-start(f32[32,2,96,16,8]{2,4,3,1,0:T(8,128)} %bitcast.367), calls=%async_computation.3 | async-start | bytes 8388608 | tf_op jit(solution)/shard_map/all_to_all | solution.py:190
  425.9 176.5 %all-reduce.7.cloned.1.call-start = ((), (), s32[]{:S(2)}) async-start(), calls=%async_computation.4 | async-start | bytes 1179648
  426.2 5.9 copy-start.2
  426.2 5.9 copy-start.16
  432.0 3.5 copy-start.4
  432.1 3.5 copy-start.10
  435.6 3.5 copy-start.7
  442.9 3.5 copy-start.14
  446.4 3.5 copy-start.12
  458.9 243.8 %all-reduce.9.cloned.1.call-start = ((), (), s32[]{:S(2)}) async-start(), calls=%async_computation.5 | async-start | bytes 131072 | tf_op jit(solution)/shard_map/psum | solution.py:207
  638.4 16.3 %copy-start.23 = (bf16[96,8,1024]{2,1,0:T(8,128)(2,1)S(1)}, bf16[96,8,1024]{2,1,0:T(8,128)(2,1)}, u32[]{:S(2)}) copy-start(bf16[96,8,1024]{2,1,0:T(8,128)(2,1)} %param.8) | copy-start | bytes 4718596
  638.4 16.3 %copy-start.29 = (f32[96,512,8]{1,2,0:T(8,128)S(1)}, f32[96,512,8]{1,2,0:T(8,128)}, u32[]{:S(2)}) copy-start(f32[96,512,8]{1,2,0:T(8,128)} %copy.124) | copy-start | bytes 4718596
  638.4 16.3 %copy-start.31 = (bf16[96,8,1024]{2,1,0:T(8,128)(2,1)S(1)}, bf16[96,8,1024]{2,1,0:T(8,128)(2,1)}, u32[]{:S(2)}) copy-start(bf16[96,8,1024]{2,1,0:T(8,128)(2,1)} %param.9) | copy-start | bytes 4718596
  638.4 16.4 %copy-start.33 = (f32[8,1024]{1,0:T(8,128)S(1)}, f32[8,1024]{1,0:T(8,128)}, u32[]{:S(2)}) copy-start(f32[8,1024]{1,0:T(8,128)} %copy-done.32) | copy-start | bytes 98308
  638.4 16.4 %copy-start.35 = (f32[8,1024]{1,0:T(8,128)S(1)}, f32[8,1024]{1,0:T(8,128)}, u32[]{:S(2)}) copy-start(f32[8,1024]{1,0:T(8,128)} %copy-done.34) | copy-start | bytes 98308
  638.5 16.4 %copy-start.44 = (f32[96]{0:T(128)S(1)}, f32[96]{0:T(128)}, u32[]{:S(2)}) copy-start(f32[96]{0:T(128)} %param.10) | copy-start | bytes 1156
  654.8 15.9 %copy-start.28 = (f32[96,512,8]{1,2,0:T(8,128)S(1)}, f32[96,512,8]{1,2,0:T(8,128)}, u32[]{:S(2)}) copy-start(f32[96,512,8]{1,2,0:T(8,128)} %copy.111) | copy-start | bytes 4718596
  654.8 15.9 %copy-start.42 = (f32[96]{0:T(128)S(1)}, f32[96]{0:T(128)}, u32[]{:S(2)}) copy-start(f32[96]{0:T(128)} %param.11) | copy-start | bytes 1156
  (4 other events, 4.2 us)
Sparse Core Ops, SparseCore 0:
  46.3 38.6 all-reduce.10
  459.1 143.3 all-reduce.6
  670.9 31.8 all-reduce.8
where the time goes:
time: 725 us; the launch traced here: 715 us
  waiting for transfers between devices  264 us (36%)
  matrix products  227 us (31%)
  local copies, waits for them, and re-layouts  116 us (16%)
  blocking collectives  54.1 us (7%)
  starting transfers between devices  20.8 us (3%)
  other arithmetic  17.5 us (2%)
  between operations  15.1 us (2%)
    dot_general x48, matrix products, contract(): return jnp.einsum(form, left, right, precision=highest)  227 us
    unnamed x4, waiting for transfers between devices  144 us
    psum x1, waiting for transfers between devices, per_device(): lax.psum((jnp.sum(tok_val, axis=0), jnp.sum(tok_val * tok_val, axis=0)),...  41.2 us
    all_to_all x1, waiting for transfers between devices, per_device(): lax.all_to_all(send_field, ('lat', 'grp'), split_axis=0, concat_axis=3, t...  34 us
    all_gather x1, blocking collectives, per_device(): lax.all_gather(b_in, 'grp', axis=0, tiled=True)  27.9 us
    another operation x8, local copies, waits for them, and re-layouts, lat_inverse(): return jnp.stack([out_real * scale, out_imag * scale])  24.5 us
    all_to_all x1, waiting for transfers between devices, per_device(): lax.all_to_all(spec_grad[None], ('lat', 'grp'), split_axis=3, concat_axis...  17.3 us
    psum x1, waiting for transfers between devices, per_device(): lax.psum((jnp.sum(dnorm, axis=0), jnp.sum(dnorm * normed, axis=0)), 'grp')  15.7 us
  transfers between devices with their start and end apart: 7, of which 6 were waited for; matrix products, arithmetic and copies ran while one was open for 27% of the time, Pallas kernels for 0%

commit v1 on v0

--- a/solution.py
+++ b/solution.py
@@ -186,7 +186,15 @@
     send_field = regroup_rows(back_field, lat_count, grp_count, chans)
     send_grad = regroup_rows(back_grad, lat_count, grp_count, chans)
     rows_field, rows_grad = (
-        lax.all_to_all(send_field, ("lat", "grp"), split_axis=0, concat_axis=3, tiled=True),
+        jnp.concatenate(
+            lax.all_to_all(
+                jnp.stack(jnp.split(send_field, lax.axis_size(("lat", "grp")), axis=0)),
+                ("lat", "grp"),
+                0,
+                0,
+            ),
+            axis=3,
+        ),
         lax.all_to_all(send_grad, ("lat", "grp"), split_axis=0, concat_axis=3, tiled=True),
     )
     rows_field = rows_field[0]

time: 725 us -> 783 us (1.080)
  waiting for transfers between devices: 264 us -> 300 us
  local copies, waits for them, and re-layouts: 116 us -> 138 us
    all_to_all x1, waiting for transfers between devices: 0.01 us -> 70 us  [per_device(): lax.all_to_all(send_grad, ('lat', 'grp'), split_axis=0, concat_axis=3, ti...]
    all_to_all x1, waiting for transfers between devices: 34 us -> 0.01 us  [per_device(): lax.all_to_all(jnp.stack(jnp.split(send_field, lax.axis_size(('lat', 'grp...]
    unnamed x91 -> x126, local copies, waits for them, and re-layouts: 4.63 us -> 23.7 us
  transfers between devices with their start and end apart: 7 -> 7, of which waited for: 6 -> 6; matrix products, arithmetic and copies ran while one was open for 27% -> 21% of each run, Pallas kernels for 0% -> 0%
where the time goes in v1:
time: 783 us; the launch traced here: 773 us
  waiting for transfers between devices  300 us (38%)
  matrix products  226 us (29%)
  local copies, waits for them, and re-layouts  138 us (18%)
  blocking collectives  54.1 us (7%)
  starting transfers between devices  20.6 us (3%)
  other arithmetic  19.3 us (2%)
  between operations  15.1 us (2%)
    dot_general x48, matrix products, contract(): return jnp.einsum(form, left, right, precision=highest)  226 us
    unnamed x4, waiting for transfers between devices  143 us
    all_to_all x1, waiting for transfers between devices, per_device(): lax.all_to_all(send_grad, ('lat', 'grp'), split_axis=0, concat_axis=3, ti...  70 us
    psum x1, waiting for transfers between devices, per_device(): lax.psum((jnp.sum(tok_val, axis=0), jnp.sum(tok_val * tok_val, axis=0)),...  41.2 us
    all_gather x1, blocking collectives, per_device(): lax.all_gather(b_in, 'grp', axis=0, tiled=True)  27.9 us
    another operation x8, local copies, waits for them, and re-layouts, lat_inverse(): return jnp.stack([out_real * scale, out_imag * scale])  25.9 us
    unnamed x126, local copies, waits for them, and re-layouts  23.7 us
    all_to_all x1, waiting for transfers between devices, per_device(): lax.all_to_all(spec_grad[None], ('lat', 'grp'), split_axis=3, concat_axis...  17.3 us
  transfers between devices with their start and end apart: 7, of which 6 were waited for; matrix products, arithmetic and copies ran while one was open for 21% of the time, Pallas kernels for 0%

profile of v1, /device:TPU:0, one launch (start us, length us, event | category | flops | bytes accessed | tf_op | source)
XLA Modules:
  0.0 773.2 jit_solution(6496265243863393427)
XLA Ops:
  7.2 12.5 %multiply_bitcast_fusion.2 = f32[1,1,96,512,8]{3,2,4,1,0:T(8,128)S(1)} fusion(bf16[96,8,1024]{2,1,0:T(8,128)(2,1)} %param.9), kind=kOutput, calls=%fused_computation.130 | convolution fusion | flops 4839571456 | bytes 3145728 | tf_op jit(solution)/shard_map/crn,nm->cmr/dot_general | solution.py:13
  19.7 11.4 %multiply_bitcast_fusion.3 = f32[1,1,96,512,8]{3,2,4,1,0:T(8,128)S(1)} fusion(bf16[96,8,1024]{2,1,0:T(8,128)(2,1)S(1)} %copy-done.31), kind=kOutput, calls=%fused_computation.131 | convolution fusion | flops 4839571456 | bytes 3145728 | tf_op jit(solution)/shard_map/crn,nm->cmr/dot_general | solution.py:13
  31.5 3.5 copy.146
  35.1 7.5 all-to-all-start.2
  43.9 41.2 %all-reduce.11.cloned.1.call-done = (f32[8,1024]{1,0:T(8,128)}, f32[8,1024]{1,0:T(8,128)}) async-done(((f32[8,1024]{1,0:T(8,128)}, f32[8,1024]{1,0:T(8,128)}), (f32[8,1024]{1,0:T(8,128)}, f32[8,1024]{1,0:T(8,128)})) %all-reduce.11.cloned.1.call-update) | async-done | bytes 65552 | tf_op jit(solution)/shard_map/psum | solution.py:126
  87.0 14.2 %multiply_bitcast_fusion.4 = f32[1,96,512,8]{2,1,3,0:T(8,128)S(1)} fusion(f32[96,8,1024]{2,1,0:T(8,128)S(1)} %fusion.6), kind=kOutput, calls=%fused_computation.136 | convolution fusion | flops 4839571456 | bytes 4718592 | tf_op jit(solution)/shard_map/crn,nm->cmr/dot_general | solution.py:13
  101.2 13.8 %multiply_bitcast_fusion.5 = f32[1,96,512,8]{2,1,3,0:T(8,128)S(1)} fusion(f32[96,8,1024]{2,1,0:T(8,128)S(1)} %fusion.6), kind=kOutput, calls=%fused_computation.137 | convolution fusion | flops 4839571456 | bytes 4718592 | tf_op jit(solution)/shard_map/crn,nm->cmr/dot_general | solution.py:13
  115.3 3.6 copy.129
  119.0 17.3 %all-to-all-done.2 = f32[1,2,96,512,8]{2,4,1,0,3:T(8,128)} async-done(((f32[1,2,96,512,8]{2,4,1,0,3:T(8,128)}), f32[1,2,96,512,8]{2,4,1,0,3:T(8,128)}, u32[]{:S(2)}, u32[]{:S(2)}) %all-to-all-start.2) | async-done | bytes 3145760 | tf_op jit(solution)/shard_map/all_to_all | solution.py:140
  136.2 4.2 all-to-all-start
  140.5 27.9 %all_gather.13 = f32[4,2,96]{2,1,0:T(2,128)S(1)} all-gather(f32[1,2,96]{2,1,0:T(2,128)S(1)} %copy-done.40), channel_id=1, replica_groups=mesh['lat'=8,'grp'=4] {'grp'}, dimensions={0}, use_global_device_ids=true | all-gather | bytes 3840 | tf_op jit(solution)/shard_map/all_gather | solution.py:146
  168.4 5.7 all_gather.15
  174.1 6.7 all_gather.12
  180.7 13.8 %all_gather.14 = f32[4,2,96,96]{3,2,0,1:T(8,128)} all-gather(f32[1,2,96,96]{3,2,0,1:T(8,128)S(1)} %bitcast.532), channel_id=1, replica_groups=mesh['lat'=8,'grp'=4] {'grp'}, dimensions={0}, use_global_device_ids=true | all-gather | bytes 368640 | tf_op jit(solution)/shard_map/all_gather | solution.py:147
  195.2 4.9 copy.229
  212.2 3.6 reshape.143
  221.7 12.5 %all-to-all-done = f32[1,2,96,512,8]{2,4,1,0,3:T(8,128)} async-done(((f32[1,2,96,512,8]{2,4,1,0,3:T(8,128)}), f32[1,2,96,512,8]{2,4,1,0,3:T(8,128)}, u32[]{:S(2)}, u32[]{:S(2)}) %all-to-all-start) | async-done | bytes 3145760 | tf_op jit(solution)/shard_map/all_to_all | solution.py:139
  234.2 4.9 copy.230
  277.9 3.9 copy_select_fusion.1
  287.3 3.7 fusion.26
  320.0 3.5 stack.154
  326.7 3.7 stack.153
  330.4 3.4 copy.140
  333.8 4.0 add_select_fusion.2
  337.9 3.4 add_bitcast_fusion
  349.3 4.3 copy.151
  353.7 3.6 reshape.145
  367.9 3.4 stack.193
  374.5 3.4 stack.192
  382.5 4.2 all-to-all-start.3
  410.5 70.0 %all-to-all-done.3 = f32[32,2,96,16,8]{2,4,3,1,0:T(8,128)} async-done(((f32[32,2,96,16,8]{2,4,3,1,0:T(8,128)}), f32[32,2,96,16,8]{2,4,3,1,0:T(8,128)}, u32[]{:S(2)}, u32[]{:S(2)}) %all-to-all-start.3) | async-done | bytes 3145760 | tf_op jit(solution)/shard_map/all_to_all | solution.py:198
  480.5 4.2 all-to-all-start.1
  485.0 5.8 fusion.127
  490.8 3.5 fusion.124
  494.4 3.4 fusion.136
  497.8 3.8 fusion.141
  501.7 3.5 fusion.159
  505.2 3.5 fusion.165
  508.7 3.6 fusion.183
  512.3 3.4 fusion.173
  517.8 143.4 %all-reduce.7.cloned.1.call-done = f32[32,4608]{1,0:T(8,128)} async-done(((f32[32,4608]{1,0:T(8,128)}), f32[32,4608]{1,0:T(8,128)}) %all-reduce.7.cloned.1.call-update) | async-done | bytes 589840
  662.7 3.9 fusion.396
  671.5 15.6 %fusion.38 = f32[96,8,1024]{2,1,0:T(8,128)} fusion(f32[96,512,8]{1,2,0:T(8,128)} %copy.156), kind=kOutput, calls=%fused_computation.56 | convolution fusion | flops 4839178240 | bytes 4718592 | tf_op jit(solution)/shard_map/cmr,mn->crn/dot_general | solution.py:13
  697.2 15.7 %fusion.40 = f32[96,8,1024]{2,1,0:T(8,128)} fusion(f32[96,512,8]{1,2,0:T(8,128)} %copy.143), kind=kOutput, calls=%fused_computation.58 | convolution fusion | flops 4839178240 | bytes 4718592 | tf_op jit(solution)/shard_map/cmr,mn->crn/dot_general | solution.py:13
  713.0 15.9 %fusion.395 = (f32[8,1024]{1,0:T(8,128)}, f32[8,1024]{1,0:T(8,128)}, f32[96,8,1024]{2,1,0:T(8,128)}) fusion(f32[8,1024]{1,0:T(8,128)S(1)} %copy-done.36, f32[8,1024]{1,0:T(8,128)S(1)} %copy-done.34, bf16[96,8,1024]{2,1,0:T(8,128)(2,1)S(1)} %copy-done.22, f32[96]{0:T(128)S(1)} %copy-done.45, f32[96,8,1024]{2,1,0:T(8,128)S(1)} %copy-done.46, ...), kind=kOutput, calls=%fused_computation.385 | convolution fusion | flops 4847812608 | bytes 11141504 | tf_op jit(solution)/shard_map/cmr,mn->crn/dot_general | solution.py:13
  729.0 16.3 %fusion.11 = bf16[96,8,1024]{2,1,0:T(8,128)(2,1)} fusion(bf16[96,8,1024]{2,1,0:T(8,128)(2,1)S(1)} %copy-done.22, f32[96,8,1024]{2,1,0:T(8,128)} %fusion.40, f32[96,512,8]{1,2,0:T(8,128)S(1)} %copy-done.30, f32[96]{0:T(128)S(1)} %copy-done.43, f32[96]{0:T(128)S(1)} %copy-done.45, f32[8,1024]{1,0:T(8,128)S(1)} %copy-done.36, f32[8,1024]{1,0:T(8,128)S(1)} %copy-done.34), kind=kOutput, calls=%fused_computation.21 | convolution fusion | flops 4847042560 | bytes 7930624 | tf_op jit(solution)/shard_map/cmr,mn->crn/dot_general | solution.py:13
  745.2 15.7 %all-reduce.9.cloned.1.call-done = (f32[8,1024]{1,0:T(8,128)}, f32[8,1024]{1,0:T(8,128)}) async-done(((f32[8,1024]{1,0:T(8,128)}, f32[8,1024]{1,0:T(8,128)}), (f32[8,1024]{1,0:T(8,128)}, f32[8,1024]{1,0:T(8,128)})) %all-reduce.9.cloned.1.call-update) | async-done | bytes 65552 | tf_op jit(solution)/shard_map/psum | solution.py:215
  761.7 4.5 fusion.1
  (204 shorter events, 168.4 us)
Async XLA Ops:
  7.2 12.5 %copy-start.31 = (bf16[96,8,1024]{2,1,0:T(8,128)(2,1)S(1)}, bf16[96,8,1024]{2,1,0:T(8,128)(2,1)}, u32[]{:S(2)}) copy-start(bf16[96,8,1024]{2,1,0:T(8,128)(2,1)} %param.9) | copy-start | bytes 4718596
  35.1 7.7 copy-start.21
  35.1 51.4 %copy-start.42 = (f32[96]{0:T(128)S(1)}, f32[96]{0:T(128)}, u32[]{:S(2)}) copy-start(f32[96]{0:T(128)} %param.11) | copy-start | bytes 1156
  35.1 51.4 %copy-start.44 = (f32[96]{0:T(128)S(1)}, f32[96]{0:T(128)}, u32[]{:S(2)}) copy-start(f32[96]{0:T(128)} %param.10) | copy-start | bytes 1156
  35.1 101.2 %all-to-all-start.2 = ((f32[1,2,96,512,8]{2,4,1,0,3:T(8,128)}), f32[1,2,96,512,8]{2,4,1,0,3:T(8,128)}, u32[]{:S(2)}, u32[]{:S(2)}) async-start(f32[1,2,96,512,8]{2,4,1,0,3:T(8,128)} %copy.146), calls=%async_computation.2 | async-start | bytes 8388608 | tf_op jit(solution)/shard_map/all_to_all | solution.py:140
  42.5 42.5 %all-reduce.11.cloned.1.call-start = ((), (), s32[]{:S(2)}) async-start(), calls=%async_computation.6 | async-start | bytes 131072 | tf_op jit(solution)/shard_map/psum | solution.py:126
  118.9 21.5 %copy-start.40 = (f32[1,2,96]{2,1,0:T(2,128)S(1)}, f32[1,2,96]{2,1,0:T(2,128)}, u32[]{:S(2)}) copy-start(f32[1,2,96]{2,1,0:T(2,128)} %param.13) | copy-start | bytes 2308
  118.9 49.4 %copy-start.41 = (f32[1,2,96]{2,1,0:T(2,128)S(1)}, f32[1,2,96]{2,1,0:T(2,128)}, u32[]{:S(2)}) copy-start(f32[1,2,96]{2,1,0:T(2,128)} %param.15) | copy-start | bytes 2308
  119.0 55.1 %copy-start.37 = (f32[1,2,96,96]{3,2,1,0:T(8,128)S(1)}, f32[1,2,96,96]{3,2,1,0:T(8,128)}, u32[]{:S(2)}) copy-start(f32[1,2,96,96]{3,2,1,0:T(8,128)} %param.12) | copy-start | bytes 221188
  119.0 61.8 %copy-start.38 = (f32[1,2,96,96]{3,2,1,0:T(8,128)S(1)}, f32[1,2,96,96]{3,2,1,0:T(8,128)}, u32[]{:S(2)}) copy-start(f32[1,2,96,96]{3,2,1,0:T(8,128)} %param.14) | copy-start | bytes 221188
  136.2 97.9 %all-to-all-start = ((f32[1,2,96,512,8]{2,4,1,0,3:T(8,128)}), f32[1,2,96,512,8]{2,4,1,0,3:T(8,128)}, u32[]{:S(2)}, u32[]{:S(2)}) async-start(f32[1,2,96,512,8]{2,4,1,0,3:T(8,128)} %copy.129), calls=%async_computation | async-start | bytes 8388608 | tf_op jit(solution)/shard_map/all_to_all | solution.py:139
  260.1 2.3 copy-start.3
  260.1 2.3 copy-start.39
  270.6 2.4 copy-start.27
  273.0 4.5 copy-start
  275.5 2.3 copy-start.26
  281.8 3.3 copy-start.15
  287.3 3.7 copy-start.10
  309.4 3.2 copy-start.17
  314.3 2.9 copy-start.19
  330.4 3.5 copy-start.1
  330.4 3.4 copy-start.13
  333.8 4.0 copy-start.25
  337.8 3.5 copy-start.8
  337.8 3.4 copy-start.24
  357.2 3.2 copy-start.18
  362.1 2.9 copy-start.20
  378.0 2.2 copy-start.28
  382.5 97.9 %all-to-all-start.3 = ((f32[32,2,96,16,8]{2,4,3,1,0:T(8,128)}), f32[32,2,96,16,8]{2,4,3,1,0:T(8,128)}, u32[]{:S(2)}, u32[]{:S(2)}) async-start(f32[32,2,96,16,8]{2,4,3,1,0:T(8,128)} %bitcast.525), calls=%async_computation.3 | async-start | bytes 8388608 | tf_op jit(solution)/shard_map/all_to_all | solution.py:198
  480.5 206.6 %all-to-all-start.1 = ((f32[32,1,2,96,16,8]{3,5,4,2,1,0:T(8,128)}), f32[32,1,2,96,16,8]{3,5,4,2,1,0:T(8,128)}, u32[]{:S(2)}, u32[]{:S(2)}) async-start(f32[32,1,2,96,16,8]{3,5,4,2,1,0:T(8,128)} %fusion.210), calls=%async_computation.1 | async-start | bytes 8388608 | tf_op jit(solution)/shard_map/all_to_all | solution.py:190
  484.7 176.5 %all-reduce.7.cloned.1.call-start = ((), (), s32[]{:S(2)}) async-start(), calls=%async_computation.4 | async-start | bytes 1179648
  484.9 5.9 copy-start.2
  484.9 5.9 copy-start.16
  490.8 3.5 copy-start.4
  490.8 3.5 copy-start.9
  494.4 3.5 copy-start.7
  501.7 3.5 copy-start.14
  505.2 3.5 copy-start.11
  517.7 243.2 %all-reduce.9.cloned.1.call-start = ((), (), s32[]{:S(2)}) async-start(), calls=%async_computation.5 | async-start | bytes 131072 | tf_op jit(solution)/shard_map/psum | solution.py:215
  697.2 15.8 %copy-start.22 = (bf16[96,8,1024]{2,1,0:T(8,128)(2,1)S(1)}, bf16[96,8,1024]{2,1,0:T(8,128)(2,1)}, u32[]{:S(2)}) copy-start(bf16[96,8,1024]{2,1,0:T(8,128)(2,1)} %param.8) | copy-start | bytes 4718596
  697.2 15.8 %copy-start.29 = (f32[96,512,8]{1,2,0:T(8,128)S(1)}, f32[96,512,8]{1,2,0:T(8,128)}, u32[]{:S(2)}) copy-start(f32[96,512,8]{1,2,0:T(8,128)} %copy.155) | copy-start | bytes 4718596
  697.2 15.8 %copy-start.32 = (bf16[96,8,1024]{2,1,0:T(8,128)(2,1)S(1)}, bf16[96,8,1024]{2,1,0:T(8,128)(2,1)}, u32[]{:S(2)}) copy-start(bf16[96,8,1024]{2,1,0:T(8,128)(2,1)} %param.9) | copy-start | bytes 4718596
  697.2 15.8 %copy-start.34 = (f32[8,1024]{1,0:T(8,128)S(1)}, f32[8,1024]{1,0:T(8,128)}, u32[]{:S(2)}) copy-start(f32[8,1024]{1,0:T(8,128)} %copy-done.33) | copy-start | bytes 98308
  697.2 15.8 %copy-start.36 = (f32[8,1024]{1,0:T(8,128)S(1)}, f32[8,1024]{1,0:T(8,128)}, u32[]{:S(2)}) copy-start(f32[8,1024]{1,0:T(8,128)} %copy-done.35) | copy-start | bytes 98308
  697.2 15.8 %copy-start.45 = (f32[96]{0:T(128)S(1)}, f32[96]{0:T(128)}, u32[]{:S(2)}) copy-start(f32[96]{0:T(128)} %param.10) | copy-start | bytes 1156
  697.2 15.8 %copy-start.46 = (f32[96,8,1024]{2,1,0:T(8,128)S(1)}, f32[96,8,1024]{2,1,0:T(8,128)}, u32[]{:S(2)}) copy-start(f32[96,8,1024]{2,1,0:T(8,128)} %fusion.38) | copy-start | bytes 9437188
  713.0 15.9 %copy-start.30 = (f32[96,512,8]{1,2,0:T(8,128)S(1)}, f32[96,512,8]{1,2,0:T(8,128)}, u32[]{:S(2)}) copy-start(f32[96,512,8]{1,2,0:T(8,128)} %copy.142) | copy-start | bytes 4718596
  713.0 15.9 %copy-start.43 = (f32[96]{0:T(128)S(1)}, f32[96]{0:T(128)}, u32[]{:S(2)}) copy-start(f32[96]{0:T(128)} %param.11) | copy-start | bytes 1156
  (6 other events, 9.4 us)
Sparse Core Ops, SparseCore 0:
  46.3 38.6 all-reduce.10
  517.8 143.3 all-reduce.6
  729.1 31.7 all-reduce.8
